TPU v7x, 32 devices: a whole 2x2x4 slice. The times are simulated.
32 devices in a mesh: dp: 4 (over y, x), seq: 8 (over z, core).
Axes of the slice: x: 2, y: 2, z: 4, core: 2. Of those that a mesh axis runs over, the one named last changes fastest.
Arguments:
- student_x: bfloat16 [4096, 4096], P(('dp', 'seq')), parts along dimension 0, may hold values from -60 to 60
- student_z: bfloat16 [4096, 4096], P(('dp', 'seq')), parts along dimension 0, may hold values from -6 to 6
- student_b: bfloat16 [4096, 1024], P(('dp', 'seq')), parts along dimension 0, may hold values from -0.5 to 0.5
- student_c: bfloat16 [4096, 1024], P(('dp', 'seq')), parts along dimension 0, may hold values from -6 to 6
- step_size: float32 [64, 4096], P(None, ('dp', 'seq')), parts along dimension 1, may hold values from 0 to 1
- decay_rate: float32 [64], replicated, may hold values from 0.5 to 2
- norm_gain: float32 [4096], replicated, may hold values from 0.5 to 1.5
- teacher_q: bfloat16 [4096, 4096], P(('dp', 'seq')), parts along dimension 0, may hold values from -140 to 140
- teacher_k: bfloat16 [4096, 1024], P(('dp', 'seq')), parts along dimension 0, may hold values from -7 to 7
- teacher_v: bfloat16 [4096, 1024], P(('dp', 'seq')), parts along dimension 0, may hold values from -6 to 6
Outputs:
- student_out: bfloat16 [4096, 4096], P(('dp', 'seq')), parts along dimension 0
- teacher_out: bfloat16 [4096, 4096], P(('dp', 'seq')), parts along dimension 0
There are 4 independent parts, one for each index of `dp`. A program takes and returns all parts, laid end to end along the dimension named above; an argument that names none is the same for every part. Nothing has to cross between parts.
All inputs are finite; a program needn't handle non-finite values.
Results may differ from a plain program's by a relative error of at most 0.0075.
Values may be sent and summed in bfloat16 or wider, within the bound.
A program may use at most 256 MiB of HBM per device.

v0:
```python
import math
import jax
import jax.numpy as jnp
from jax import lax
from jax.sharding import PartitionSpec as P

GROUPS = 8
HEAD_SIZE = 128
BLOCK = 128
epsilon_norm = 1e-05
masked_score = -1e30
HIGHEST = lax.Precision.HIGHEST


def entering(array, axis, combine, identity):
    devices, place = (lax.axis_size(axis), lax.axis_index(axis))
    everything = jax.tree.map(
        lambda part, kind: lax.all_gather(part.astype(kind), axis),
        array,
        (jnp.bfloat16, jnp.bfloat16),
    )
    start = jax.tree.map(
        lambda part, zero: jnp.broadcast_to(jnp.asarray(zero, part.dtype), part.shape),
        array,
        identity,
    )

    def step(k, before):
        reached = k < place
        new = combine(
            before, jax.tree.map(lambda part, own: part[k].astype(own.dtype), everything, array)
        )
        return jax.tree.map(lambda a, b: jnp.where(reached, a, b), new, before)

    return lax.fori_loop(0, devices, step, start)


def block_pass(carry_state, block_inputs, decay_rate, group_count):
    x_block, b_block, c_block, step_block = block_inputs
    block_rows = x_block.shape[0]
    head_count = step_block.shape[0]
    state_dim = b_block.shape[1] // group_count
    per_group = head_count // group_count
    head_width = x_block.shape[1] // head_count
    log_decay = -step_block * decay_rate[:, None]
    running = jnp.cumsum(log_decay, axis=1)
    b_three = b_block.reshape(block_rows, group_count, state_dim)
    c_three = c_block.reshape(block_rows, group_count, state_dim)
    x_four = x_block.reshape(block_rows, group_count, per_group, head_width)
    products = jnp.einsum("tgn,sgn->gts", c_three, b_three, preferred_element_type=jnp.float32)
    lower_mask = jnp.arange(block_rows)[:, None] >= jnp.arange(block_rows)[None, :]
    spread = running[:, :, None] - running[:, None, :]
    factor = jnp.exp(jnp.where(lower_mask[None], spread, masked_score))
    weights = (
        products[:, None] * factor.reshape(group_count, per_group, block_rows, block_rows)
    ).astype(jnp.bfloat16)
    local_out = jnp.einsum("gkts,sgkp->tgkp", weights, x_four, preferred_element_type=jnp.float32)
    state_four = carry_state.reshape(group_count, per_group, head_width, state_dim)
    carried = jnp.einsum(
        "tgn,gkpn->tgkp", c_three.astype(jnp.float32), state_four, precision=HIGHEST
    )
    carried = carried * jnp.exp(running).T.reshape(block_rows, group_count, per_group, 1)
    tail_decay = jnp.exp(running[:, -1:] - running)
    scaled = x_four.astype(jnp.float32) * tail_decay.T.reshape(
        block_rows, group_count, per_group, 1
    )
    fresh_state = jnp.einsum(
        "sgkp,sgn->gkpn", scaled, b_three.astype(jnp.float32), precision=HIGHEST
    )
    new_state = (
        jnp.exp(running[:, -1]).reshape(group_count, per_group, 1, 1) * state_four + fresh_state
    )
    combined = (local_out + carried).reshape(block_rows, head_count * head_width)
    return (new_state.reshape(head_count, head_width, state_dim), combined)


def attend_block(fold_carry, query_four, key_block, value_block, key_start, query_pos, score_scale):
    row_max, row_total, weighted = fold_carry
    key_rows = key_block.shape[0]
    kv_count = query_four.shape[1]
    head_width = query_four.shape[3]
    keys_three = key_block.reshape(key_rows, kv_count, head_width)
    values_three = value_block.reshape(key_rows, kv_count, head_width)
    scores = (
        jnp.einsum("qgkd,sgd->qgks", query_four, keys_three, preferred_element_type=jnp.float32)
        * score_scale
    )
    key_pos = key_start + jnp.arange(key_rows)
    visible = (key_pos[None, :] <= query_pos[:, None])[:, None, None, :]
    masked = jnp.where(visible, scores, masked_score)
    new_max = jnp.maximum(row_max, jnp.max(masked, axis=3))
    shrink = jnp.exp(row_max - new_max)
    probabilities = jnp.where(visible, jnp.exp(masked - new_max[..., None]), 0.0)
    row_total = row_total * shrink + jnp.sum(probabilities, axis=3)
    update = jnp.einsum(
        "qgks,sgd->qgkd",
        probabilities.astype(jnp.bfloat16),
        values_three,
        preferred_element_type=jnp.float32,
    )
    weighted = weighted * shrink[..., None] + update
    return (new_max, row_total, weighted)


def on_device(
    student_x,
    student_z,
    student_b,
    student_c,
    step_size,
    decay_rate,
    norm_gain,
    teacher_q,
    teacher_k,
    teacher_v,
):
    tokens, width = student_x.shape
    head_count = step_size.shape[0]
    head_width = width // head_count
    group_count = GROUPS
    per_group = head_count // group_count
    state_dim = student_b.shape[1] // group_count
    block_count = tokens // BLOCK
    my_index = lax.axis_index("seq")
    blocks_in = (
        student_x.reshape(block_count, BLOCK, width),
        student_b.reshape(block_count, BLOCK, group_count * state_dim),
        student_c.reshape(block_count, BLOCK, group_count * state_dim),
        step_size.reshape(head_count, block_count, BLOCK).transpose(1, 0, 2),
    )

    def advance(carry_state, block_inputs):
        return block_pass(carry_state, block_inputs, decay_rate, group_count)

    zero_state = jnp.zeros((head_count, head_width, state_dim), jnp.float32)
    local_state, block_outs = lax.scan(advance, zero_state, blocks_in)
    cum_device = jnp.cumsum(-step_size * decay_rate[:, None], axis=1)
    device_decay = jnp.exp(cum_device[:, -1])

    def combine(earlier, following):
        return (earlier[0] * following[0], following[0][:, None, None] * earlier[1] + following[1])

    identity = (jnp.ones_like(device_decay), jnp.zeros_like(local_state))
    incoming = entering((device_decay, local_state), "seq", combine, identity)[1]
    ratio = teacher_q.shape[1] // teacher_k.shape[1]
    kv_count = teacher_k.shape[1] // HEAD_SIZE
    query_four = teacher_q.reshape(tokens, kv_count, ratio, HEAD_SIZE)
    query_pos = my_index * tokens + jnp.arange(tokens)
    score_scale = 1.0 / math.sqrt(HEAD_SIZE)
    start_carry = (
        jnp.full((tokens, kv_count, ratio), masked_score, jnp.float32),
        jnp.zeros((tokens, kv_count, ratio), jnp.float32),
        jnp.zeros((tokens, kv_count, ratio, HEAD_SIZE), jnp.float32),
    )
    key_piece = lax.all_gather(teacher_k, "seq", axis=0, tiled=True)
    value_piece = lax.all_gather(teacher_v, "seq", axis=0, tiled=True)
    piece_rows = key_piece.shape[0]
    sub_rows = math.gcd(piece_rows, 512)

    def visit_block(block_index, current):
        key_block = lax.dynamic_slice_in_dim(key_piece, block_index * sub_rows, sub_rows, 0)
        value_block = lax.dynamic_slice_in_dim(value_piece, block_index * sub_rows, sub_rows, 0)
        return attend_block(
            current,
            query_four,
            key_block,
            value_block,
            block_index * sub_rows,
            query_pos,
            score_scale,
        )

    final_carry = lax.fori_loop(0, piece_rows // sub_rows, visit_block, start_carry)
    _, row_total, weighted = final_carry
    teacher_out = (
        (weighted / row_total[..., None])
        .reshape(tokens, kv_count * ratio * HEAD_SIZE)
        .astype(jnp.bfloat16)
    )
    c_three = student_c.reshape(tokens, group_count, state_dim).astype(jnp.float32)
    in_four = incoming.reshape(group_count, per_group, head_width, state_dim)
    carried_in = jnp.einsum("tgn,gkpn->tgkp", c_three, in_four, precision=HIGHEST)
    carried_in = carried_in * jnp.exp(cum_device).T.reshape(tokens, group_count, per_group, 1)
    combined = block_outs.reshape(tokens, group_count, per_group, head_width) + carried_in
    gated_out = combined.reshape(tokens, head_count, head_width) * jax.nn.silu(
        student_z.astype(jnp.float32)
    ).reshape(tokens, head_count, head_width)
    mean_square = jnp.mean(gated_out * gated_out, axis=2, keepdims=True)
    normed = (
        gated_out
        * lax.rsqrt(mean_square + epsilon_norm)
        * norm_gain.reshape(1, head_count, head_width)
    )
    student_out = normed.reshape(tokens, width).astype(jnp.bfloat16)
    return (student_out, teacher_out)


def solution(mesh):
    return jax.shard_map(
        on_device,
        mesh=mesh,
        in_specs=(
            P(("dp", "seq"), None),
            P(("dp", "seq"), None),
            P(("dp", "seq"), None),
            P(("dp", "seq"), None),
            P(None, ("dp", "seq")),
            P(),
            P(),
            P(("dp", "seq"), None),
            P(("dp", "seq"), None),
            P(("dp", "seq"), None),
        ),
        out_specs=(P(("dp", "seq"), None), P(("dp", "seq"), None)),
        check_vma=False,
    )
```

profile of v0, /device:TPU:0, one launch (start us, length us, event | category | flops | bytes accessed | tf_op | source)
XLA Modules:
  0.0 190.1 jit_solution(6066163782654913500)
XLA Ops:
  7.2 1.9 copy.44
  9.2 1.8 copy.46
  13.3 2.2 %add_convert_fusion = bf16[8,8,64,128]{3,2,1,0:T(8,128)(2,1)} fusion(bf16[128,8,8,64]{0,3,2,1:T(8,128)(2,1)S(1)} %bitcast.130, f32[128,8,8]{0,2,1:T(8,128)S(1)} %get-tuple-element.366, f32[8,8]{1,0:T(8,128)S(1)} %mul.192, bf16[128,8,128,1]{2,1,0,3:T(8,128)(2,1)S(1)} %bitcast.135), kind=kOutput, calls=%fused_computation.42 | convolution fusion | flops 807403520 | bytes 2392320 | tf_op jit(solution)/shard_map/while/body/eval_jaxpr/sgkp,sgn->gkpn/dot_general | solution.py:67
  17.3 19.1 %all-reduce = bf16[512]{0:T(512)(128)(2,1)S(1)} all-reduce(bf16[512]{0:T(512)(128)(2,1)S(1)} %dynamic-update-slice), channel_id=2, replica_groups=mesh['dp'=4,'seq'=8] {'seq'}, use_global_device_ids=true, to_apply=%add | all-reduce | flops 512 | bytes 2048
  39.4 2.3 %copy.45 = bf16[128,4096]{0,1:T(8,128)(2,1)} copy(bf16[128,4096]{1,0:T(8,128)(2,1)} %param.21) | data formatting | bytes 2097152 | tf_op args[7]
  41.7 1.6 copy.47
  43.4 1.4 fusion.36
  44.8 2.3 %fusion.34 = f32[8,8,64,128]{3,2,1,0:T(8,128)} fusion(bf16[128,8,128,1]{2,1,0,3:T(8,128)(2,1)S(1)} %bitcast.127), kind=kOutput, calls=%fused_computation.52 | convolution fusion | flops 805306368 | bytes 2359296 | tf_op jit(solution)/shard_map/while/body/eval_jaxpr/tgn,gkpn->tgkp/dot_general | solution.py:59
  47.1 3.2 %fusion.18 = f32[8,8,128,64]{2,3,1,0:T(8,128)} fusion(bf16[128,8,8,64]{0,3,2,1:T(8,128)(2,1)S(1)} %bitcast.131, f32[8,8,128]{2,1,0:T(8,128)S(1)} %bitcast.134, f32[8,128,128]{2,1,0:T(8,128)S(1)} %fusion.36, pred[128,128]{1,0:T(8,128)(4,1)S(1)} %iota_compare_fusion), kind=kOutput, calls=%fused_computation.31 | convolution fusion | flops 138412032 | bytes 3719168 | tf_op jit(solution)/shard_map/while/body/eval_jaxpr/gkts,sgkp->tgkp/dot_general | solution.py:57
  50.4 24.1 %all-gather.9.cloned.1.call-done = bf16[1024,1024]{0,1:T(8,128)(2,1)} async-done(((bf16[128,1024]{0,1:T(8,128)(2,1)}), bf16[1024,1024]{0,1:T(8,128)(2,1)}) %all-gather.9.cloned.1.call-update) | async-done | bytes 2097168 | tf_op jit(solution)/shard_map/all_gather | solution.py:156
  74.5 37.5 %while.38 = (s32[]{:T(128)}, f32[128,8,4]{0,2,1:T(4,128)S(1)}, f32[128,8,4]{0,2,1:T(4,128)S(1)}, f32[128,8,4,128]{0,3,2,1:T(8,128)}, bf16[1024,1024]{0,1:T(8,128...) while((s32[]{:T(128)}, f32[128,8,4]{0,2,1:T(4,128)S(1)}, ...), condition=%wide.region_7.8_spmd.clone, body=%wide.region_4.7_spmd.clone.sunk | while | flops 1102664320 | bytes 70784216 | solution.py:173
  74.5 2.6 %constant_dynamic-slice_fusion.3 = (bf16[512,1024]{0,1:T(8,128)(2,1)}, bf16[512,1024]{0,1:T(8,128)(2,1)S(1)}) fusion(bf16[1024,1024]{0,1:T(8,128)(2,1)} %get-tuple-element.512, s32[]{:T(128)S(6)} %select_n.96, bf16[1024,1024]{0,1:T(8,128)(2,1)} %get-tuple-element.510), kind=kLoop, calls=%fused_computation.20.clone.1 | loop fusion | bytes 4194308 | tf_op jit(solution)/shard_map/while/body/eval_jaxpr/dynamic_slice | solution.py:162
  77.3 4.7 %fusion.68 = (f32[128,8,4]{0,2,1:T(4,128)S(1)}, f32[8,512,128,4]{2,1,3,0:T(8,128)}) fusion(pred[128,512]{0,1:T(8,128)(4,1)S(1)} %broadcast_compare_fusion.2, bf16[512,8,128,1]{0,2,3,1:T(8,128)(2,1)S(1)} %bitcast.122, bf16[128,8,4,128]{3,0,2,1:T(8,128)(2,1)S(1)} %get-tuple-element.511), kind=kOutput, calls=%fused_computation.6.clone.1 | convolution fusion | flops 543158272 | bytes 10567680 | tf_op jit(solution)/shard_map/while/body/eval_jaxpr/qgkd,sgd->qgks/dot_general | solution.py:85
  82.0 5.7 %fusion.69 = f32[128,8,4]{0,2,1:T(4,128)S(1)} fusion(f32[8,512,128,4]{2,1,3,0:T(8,128)} %get-tuple-element.457, f32[128,8,4]{0,2,1:T(4,128)S(1)} %select_maximum_fusion.2, pred[128,512]{0,1:T(8,128)(4,1)S(1)} %broadcast_compare_fusion.2), kind=kLoop, calls=%fused_computation.8.clone.1 | loop fusion | flops 10481664 | bytes 8486912 | tf_op jit(solution)/shard_map/while/body/eval_jaxpr/reduce_sum | solution.py:94
  88.9 4.6 %bitcast_add_fusion.2 = f32[128,8,4,128]{0,3,2,1:T(8,128)} fusion(f32[128,8,4,128]{0,3,2,1:T(8,128)} %get-tuple-element.497, bf16[512,8,128,1]{0,2,3,1:T(8,128)(2,1)} %bitcast.124, f32[8,512,128,4]{2,1,3,0:T(8,128)S(1)} %copy-done, f32[128,8,4]{0,2,1:T(4,128)S(1)} %select_maximum_fusion.2, pred[128,512]{0,1:T(8,128)(4,1)S(1)} %broadcast_compare_fusion.2, ...), kind=kOutput, calls=%fused_computation.11.clone.1 | convolution fusion | flops 548929536 | bytes 13729793 | tf_op jit(solution)/shard_map/while/body/eval_jaxpr/qgks,sgd->qgkd/dot_general | solution.py:95
  93.5 2.6 %constant_dynamic-slice_fusion.3 = (bf16[512,1024]{0,1:T(8,128)(2,1)}, bf16[512,1024]{0,1:T(8,128)(2,1)S(1)}) fusion(bf16[1024,1024]{0,1:T(8,128)(2,1)} %get-tuple-element.512, s32[]{:T(128)S(6)} %select_n.96, bf16[1024,1024]{0,1:T(8,128)(2,1)} %get-tuple-element.510), kind=kLoop, calls=%fused_computation.20.clone.1 | loop fusion | bytes 4194308 | tf_op jit(solution)/shard_map/while/body/eval_jaxpr/dynamic_slice | solution.py:162
  96.3 4.7 %fusion.68 = (f32[128,8,4]{0,2,1:T(4,128)S(1)}, f32[8,512,128,4]{2,1,3,0:T(8,128)}) fusion(pred[128,512]{0,1:T(8,128)(4,1)S(1)} %broadcast_compare_fusion.2, bf16[512,8,128,1]{0,2,3,1:T(8,128)(2,1)S(1)} %bitcast.122, bf16[128,8,4,128]{3,0,2,1:T(8,128)(2,1)S(1)} %get-tuple-element.511), kind=kOutput, calls=%fused_computation.6.clone.1 | convolution fusion | flops 543158272 | bytes 10567680 | tf_op jit(solution)/shard_map/while/body/eval_jaxpr/qgkd,sgd->qgks/dot_general | solution.py:85
  101.0 4.8 %fusion.69 = f32[128,8,4]{0,2,1:T(4,128)S(1)} fusion(f32[8,512,128,4]{2,1,3,0:T(8,128)} %get-tuple-element.457, f32[128,8,4]{0,2,1:T(4,128)S(1)} %select_maximum_fusion.2, pred[128,512]{0,1:T(8,128)(4,1)S(1)} %broadcast_compare_fusion.2), kind=kLoop, calls=%fused_computation.8.clone.1 | loop fusion | flops 10481664 | bytes 8486912 | tf_op jit(solution)/shard_map/while/body/eval_jaxpr/reduce_sum | solution.py:94
  107.0 5.0 %bitcast_add_fusion.2 = f32[128,8,4,128]{0,3,2,1:T(8,128)} fusion(f32[128,8,4,128]{0,3,2,1:T(8,128)} %get-tuple-element.497, bf16[512,8,128,1]{0,2,3,1:T(8,128)(2,1)} %bitcast.124, f32[8,512,128,4]{2,1,3,0:T(8,128)S(1)} %copy-done, f32[128,8,4]{0,2,1:T(4,128)S(1)} %select_maximum_fusion.2, pred[128,512]{0,1:T(8,128)(4,1)S(1)} %broadcast_compare_fusion.2, ...), kind=kOutput, calls=%fused_computation.11.clone.1 | convolution fusion | flops 548929536 | bytes 13729793 | tf_op jit(solution)/shard_map/while/body/eval_jaxpr/qgks,sgd->qgkd/dot_general | solution.py:95
  112.0 1.9 %divide_convert_fusion = bf16[128,8,4,128]{0,3,2,1:T(8,128)(2,1)S(1)} fusion(f32[128,8,4,128]{0,3,2,1:T(8,128)} %get-tuple-element.261, f32[128,8,4]{0,2,1:T(4,128)S(1)} %get-tuple-element.262), kind=kLoop, calls=%fused_computation.40 | loop fusion | flops 1048576 | bytes 3162112 | tf_op jit(solution)/shard_map/convert_element_type | solution.py:178
  113.9 1.3 copy.62
  115.3 41.9 %all-gather.5.cloned.1.call-done = bf16[8,64,64,128]{3,2,1,0:T(8,128)(2,1)} async-done(((bf16[1,64,64,128]{3,2,1,0:T(8,128)(2,1)}), bf16[8,64,64,128]{3,2,1,0:T(8,128)(2,1)}) %all-gather.5.cloned.1.call-update) | async-done | bytes 8388624 | tf_op jit(solution)/shard_map/all_gather | solution.py:18
  157.2 19.8 %while.37 = (s32[]{:T(128)}, f32[64,64,128]{2,1,0:T(8,128)S(1)}, s32[]{:T(128)}, bf16[8,64]{1,0:T(8,128)(2,1)}, bf16[8,64,64,128]{3,2,1,0:T(8,128)(2,1)}, /*index=5*/s32[]{:T(128)}, s32[]{:T(128)}) while((s32[]{:T(128)}, f32[64,64,128]{2,1,0:T(8,128)S(1)}, s32[]{:T(128)}, bf16[8,64]{1,0:T(8,128)(2,1)}, ...), condition=%wide.region_2.3_spmd.clone, body=%wide.region_1.2_spmd.clone.sunk | while | flops 2621508 | bytes 5243625 | solution.py:35
  157.9 1.8 fusion.63
  160.4 1.8 fusion.63
  162.9 1.8 fusion.63
  165.3 1.8 fusion.63
  167.8 1.8 fusion.63
  170.3 1.8 fusion.63
  172.7 1.8 fusion.63
  175.2 1.8 fusion.63
  177.0 4.3 %multiply_reduce_fusion = (f32[128,8,8]{0,2,1:T(8,128)S(1)}, f32[128,8,8,64]{0,3,2,1:T(8,128)S(1)}) fusion(bf16[128,4096]{0,1:T(8,128)(2,1)S(1)} %copy-done.1, f32[8,8,64,128]{3,2,1,0:T(8,128)S(1)} %bitcast.123, bf16[128,8,128,1]{2,1,0,3:T(8,128)(2,1)S(1)} %bitcast.128, f32[128,8,8]{0,2,1:T(8,128)S(1)} %get-tuple-element.365, ...), kind=kOutput, calls=%fused_computation.41 | convolution fusion | flops 811589632 | bytes 9764864 | tf_op jit(solution)/shard_map/tgn,gkpn->tgkp/dot_general | solution.py:182
  (69 shorter events, 17.0 us)
Async XLA Ops:
  7.2 5.3 %copy-start.2 = (bf16[128,4096]{1,0:T(8,128)(2,1)S(1)}, bf16[128,4096]{1,0:T(8,128)(2,1)}, u32[]{:S(2)}) copy-start(bf16[128,4096]{1,0:T(8,128)(2,1)} %param.14) | copy-start | bytes 3145732
  7.2 6.0 %copy-start.6 = (bf16[128,1024]{1,0:T(8,128)(2,1)S(1)}, bf16[128,1024]{1,0:T(8,128)(2,1)}, u32[]{:S(2)}) copy-start(bf16[128,1024]{1,0:T(8,128)(2,1)} %param.16) | copy-start | bytes 786436
  7.2 43.2 %all-gather.7.cloned.1.call-start = ((), (), s32[]{:S(2)}) async-start(), calls=%async_computation.1 | async-start | bytes 2359296 | tf_op jit(solution)/shard_map/all_gather | solution.py:155
  9.1 65.4 %all-gather.9.cloned.1.call-start = ((), (), s32[]{:S(2)}) async-start(), calls=%async_computation.2 | async-start | bytes 2359296 | tf_op jit(solution)/shard_map/all_gather | solution.py:156
  11.0 146.2 %all-gather.5.cloned.1.call-start = ((), (), s32[]{:S(2)}) async-start(), calls=%async_computation | async-start | bytes 9437184 | tf_op jit(solution)/shard_map/all_gather | solution.py:18
  13.1 2.5 %copy-start.4 = (bf16[128,4096]{0,1:T(8,128)(2,1)}, bf16[128,4096]{0,1:T(8,128)(2,1)S(1)}, u32[]{:S(2)}) copy-start(bf16[128,4096]{0,1:T(8,128)(2,1)S(1)} %copy.39) | copy-start | bytes 3145732
  13.1 2.5 %copy-start.8 = (u32[32]{0:T(128)S(1)}, u32[32]{0:T(128)}, u32[]{:S(2)}) copy-start(u32[32]{0:T(128)} %constant.120) | copy-start | bytes 388
  13.2 24.9 %copy-start.3 = (bf16[128,4096]{1,0:T(8,128)(2,1)S(1)}, bf16[128,4096]{1,0:T(8,128)(2,1)}, u32[]{:S(2)}) copy-start(bf16[128,4096]{1,0:T(8,128)(2,1)} %param.15) | copy-start | bytes 3145732
  43.4 3.8 %copy-start.5 = (bf16[128,4096]{0,1:T(8,128)(2,1)S(1)}, bf16[128,4096]{0,1:T(8,128)(2,1)}, u32[]{:S(2)}) copy-start(bf16[128,4096]{0,1:T(8,128)(2,1)} %copy-done.4) | copy-start | bytes 3145732
  82.0 6.9 %copy-start = (f32[8,512,128,4]{2,1,3,0:T(8,128)S(1)}, f32[8,512,128,4]{2,1,3,0:T(8,128)}, u32[]{:S(2)}) copy-start(f32[8,512,128,4]{2,1,3,0:T(8,128)} %get-tuple-element.457) | copy-start | bytes 25165828 | tf_op jit(solution)/shard_map/while
  101.0 6.0 %copy-start = (f32[8,512,128,4]{2,1,3,0:T(8,128)S(1)}, f32[8,512,128,4]{2,1,3,0:T(8,128)}, u32[]{:S(2)}) copy-start(f32[8,512,128,4]{2,1,3,0:T(8,128)} %get-tuple-element.457) | copy-start | bytes 25165828 | tf_op jit(solution)/shard_map/while
  157.2 19.8 %copy-start.1 = (bf16[128,4096]{0,1:T(8,128)(2,1)S(1)}, bf16[128,4096]{0,1:T(8,128)(2,1)}, u32[]{:S(2)}) copy-start(bf16[128,4096]{0,1:T(8,128)(2,1)} %copy.43) | copy-start | bytes 3145732
  177.0 4.3 %copy-start.7 = (f32[4096]{0:T(1024)S(1)}, f32[4096]{0:T(1024)}, u32[]{:S(2)}) copy-start(f32[4096]{0:T(1024)} %param.20) | copy-start | bytes 49156
Sparse Core Ops, SparseCore 0:
  9.6 33.5 all-gather.6
  44.8 29.6 all-gather.8
  76.1 81.0 all-gather.4
where the time goes:
time: 191 us; the launch traced here: 190 us
  waiting for transfers between devices  66.1 us (35%)
  other arithmetic  35 us (18%)
  matrix products  32.5 us (17%)
  local copies, waits for them, and re-layouts  22.5 us (12%)
  blocking collectives  19.1 us (10%)
  between operations  14.6 us (8%)
    all_gather x1, waiting for transfers between devices, entering(): lax.all_gather(part.astype(kind), axis)  41.9 us
    all_gather x1, waiting for transfers between devices, on_device(): value_piece = lax.all_gather(teacher_v, 'seq', axis=0, tiled=True)  24.1 us
    unnamed x1, blocking collectives  19.1 us
    select_n x8, other arithmetic, step(): return jax.tree.map(lambda a, b: jnp.where(reached, a, b), new, before)  14.1 us
    unnamed x28, local copies, waits for them, and re-layouts  12.8 us
    reduce_sum x2, other arithmetic, attend_block(): row_total = row_total * shrink + jnp.sum(probabilities, axis=3)  10.5 us
    dot_general x2, matrix products, attend_block(): jnp.einsum('qgks,sgd->qgkd', probabilities.astype(jnp.bfloat16), values_t...  9.59 us
    dot_general x2, matrix products, attend_block(): jnp.einsum('qgkd,sgd->qgks', query_four, keys_three, preferred_element_ty...  9.4 us
  transfers between devices with their start and end apart: 3, of which 2 were waited for; matrix products, arithmetic and copies ran while one was open for 31% of the time, Pallas kernels for 0%

commit v1 on v0

--- a/solution.py
+++ b/solution.py
@@ -153,7 +153,12 @@
         jnp.zeros((tokens, kv_count, ratio, HEAD_SIZE), jnp.float32),
     )
     key_piece = lax.all_gather(teacher_k, "seq", axis=0, tiled=True)
-    value_piece = lax.all_gather(teacher_v, "seq", axis=0, tiled=True)
+    ring = [teacher_v]
+    for hop in range(7):
+        ring.append(lax.ppermute(ring[-1], "seq", [(dev, (dev + 1) % 8) for dev in range(8)]))
+    value_piece = jnp.roll(
+        jnp.concatenate(ring[::-1], axis=0), (lax.axis_index("seq") + 1) * ring[0].shape[0], axis=0
+    )
     piece_rows = key_piece.shape[0]
     sub_rows = math.gcd(piece_rows, 512)
 

time: 191 us -> 189 us (0.990)
  the two profiles are of different devices: /device:TPU:0 before, /device:TPU:16 now
where the time goes in v1:
time: 189 us; the launch traced here: 188 us
  waiting for transfers between devices  61.1 us (32%)
  matrix products  33.1 us (18%)
  local copies, waits for them, and re-layouts  29.8 us (16%)
  other arithmetic  28.5 us (15%)
  blocking collectives  16.9 us (9%)
  between operations  15.2 us (8%)
  starting transfers between devices  3.15 us (2%)
    ppermute x7, waiting for transfers between devices, on_device(): lax.ppermute(ring[-1], 'seq', [(dev, (dev + 1) % 8) for dev in range(8)])  61.1 us
    unnamed x55, local copies, waits for them, and re-layouts  19.1 us
    unnamed x1, blocking collectives  16.9 us
    select_n x8, other arithmetic, step(): return jax.tree.map(lambda a, b: jnp.where(reached, a, b), new, before)  14.3 us
    dot_general x2, matrix products, attend_block(): jnp.einsum('qgks,sgd->qgkd', probabilities.astype(jnp.bfloat16), values_t...  9.56 us
    dot_general x2, matrix products, attend_block(): jnp.einsum('qgkd,sgd->qgks', query_four, keys_three, preferred_element_ty...  9.41 us
    reduce_sum x2, other arithmetic, attend_block(): row_total = row_total * shrink + jnp.sum(probabilities, axis=3)  9.4 us
    dynamic_slice x2, local copies, waits for them, and re-layouts, visit_block(): lax.dynamic_slice_in_dim(value_piece, block_index * sub_rows, sub_rows, 0)  5.29 us
  transfers between devices with their start and end apart: 9, of which 6 were waited for; matrix products, arithmetic and copies ran while one was open for 35% of the time, Pallas kernels for 0%

profile of v1, /device:TPU:16, one launch (start us, length us, event | category | flops | bytes accessed | tf_op | source)
XLA Modules:
  0.0 187.9 jit_solution(13286867920029367560)
XLA Ops:
  7.2 1.9 %copy.48 = bf16[128,1024]{0,1:T(8,128)(2,1)} copy(bf16[128,1024]{1,0:T(8,128)(2,1)} %param.22) | data formatting | bytes 524288 | tf_op args[8]
  13.6 2.3 %add_convert_fusion = bf16[8,8,64,128]{3,2,1,0:T(8,128)(2,1)} fusion(bf16[128,8,8,64]{0,3,2,1:T(8,128)(2,1)S(1)} %bitcast.130, f32[128,8,8]{0,2,1:T(8,128)S(1)} %get-tuple-element.366, f32[8,8]{1,0:T(8,128)S(1)} %mul.195, bf16[128,8,128,1]{2,1,0,3:T(8,128)(2,1)S(1)} %bitcast.135), kind=kOutput, calls=%fused_computation.42 | convolution fusion | flops 807403520 | bytes 2392320 | tf_op jit(solution)/shard_map/while/body/eval_jaxpr/sgkp,sgn->gkpn/dot_general | solution.py:67
  16.1 11.4 %collective-permute-done = bf16[128,1024]{0,1:T(8,128)(2,1)S(1)} collective-permute-done((bf16[128,1024]{0,1:T(8,128)(2,1)S(1)}, bf16[128,1024]{0,1:T(8,128)(2,1)S(1)}, u32[]{:S(2)}, u32[]{:S(2)}) %collective-permute-start) | collective-permute-done | bytes 262176 | tf_op jit(solution)/shard_map/ppermute | solution.py:158
  27.9 8.3 %collective-permute-done.1 = bf16[128,1024]{0,1:T(8,128)(2,1)S(1)} collective-permute-done((bf16[128,1024]{0,1:T(8,128)(2,1)S(1)}, bf16[128,1024]{0,1:T(8,128)(2,1)S(1)}, u32[]{:S(2)}, u32[]{:S(2)}) %collective-permute-start.1) | collective-permute-done | bytes 262176 | tf_op jit(solution)/shard_map/ppermute | solution.py:158
  36.2 2.5 %collective-permute-start.2 = (bf16[128,1024]{0,1:T(8,128)(2,1)S(1)}, bf16[128,1024]{0,1:T(8,128)(2,1)S(1)}, u32[]{:S(2)}, u32[]{:S(2)}) collective-permute-start(bf16[128,1024]{0,1:T(8,128)(2,1)S(1)} %collective-permute-done.1), channel_id=1, source_target_pairs={{0,1},{1,2},{2,3},{3,4},{4,5},{5,6},{6,7},{7,0},{8,9},{9,10},{10,1... | collective-permute-start | bytes 786440 | tf_op jit(solution)/shard_map/ppermute | solution.py:158
  38.7 6.3 %collective-permute-done.2 = bf16[128,1024]{0,1:T(8,128)(2,1)S(1)} collective-permute-done((bf16[128,1024]{0,1:T(8,128)(2,1)S(1)}, bf16[128,1024]{0,1:T(8,128)(2,1)S(1)}, u32[]{:S(2)}, u32[]{:S(2)}) %collective-permute-start.2) | collective-permute-done | bytes 262176 | tf_op jit(solution)/shard_map/ppermute | solution.py:158
  45.3 5.6 %collective-permute-done.3 = bf16[128,1024]{0,1:T(8,128)(2,1)} collective-permute-done((bf16[128,1024]{0,1:T(8,128)(2,1)S(1)}, bf16[128,1024]{0,1:T(8,128)(2,1)}, u32[]{:S(2)}, u32[]{:S(2)}) %collective-permute-start.3) | collective-permute-done | bytes 262176 | tf_op jit(solution)/shard_map/ppermute | solution.py:158
  55.5 16.9 %all-reduce = bf16[512]{0:T(512)(128)(2,1)S(1)} all-reduce(bf16[512]{0:T(512)(128)(2,1)S(1)} %dynamic-update-slice), channel_id=2, replica_groups=mesh['dp'=4,'seq'=8] {'seq'}, use_global_device_ids=true, to_apply=%add | all-reduce | flops 512 | bytes 2048
  74.2 2.3 %copy.47 = bf16[128,4096]{0,1:T(8,128)(2,1)} copy(bf16[128,4096]{1,0:T(8,128)(2,1)} %param.15) | data formatting | bytes 2097152 | tf_op args[1]
  77.9 3.9 %fusion.18 = f32[8,8,128,64]{2,3,1,0:T(8,128)} fusion(bf16[128,8,8,64]{0,3,2,1:T(8,128)(2,1)} %bitcast.131, f32[8,8,128]{2,1,0:T(8,128)S(1)} %bitcast.134, f32[8,128,128]{2,1,0:T(8,128)S(1)} %fusion.36, pred[128,128]{1,0:T(8,128)(4,1)S(1)} %iota_compare_fusion), kind=kOutput, calls=%fused_computation.31 | convolution fusion | flops 138412032 | bytes 3719168 | tf_op jit(solution)/shard_map/while/body/eval_jaxpr/gkts,sgkp->tgkp/dot_general | solution.py:57
  81.8 13.1 %collective-permute-done.5 = bf16[128,1024]{0,1:T(8,128)(2,1)S(1)} collective-permute-done((bf16[128,1024]{0,1:T(8,128)(2,1)}, bf16[128,1024]{0,1:T(8,128)(2,1)S(1)}, u32[]{:S(2)}, u32[]{:S(2)}) %collective-permute-start.5) | collective-permute-done | bytes 262176 | tf_op jit(solution)/shard_map/ppermute | solution.py:158
  94.9 2.3 %fusion.34 = f32[8,8,64,128]{3,2,1,0:T(8,128)} fusion(bf16[128,8,128,1]{2,1,0,3:T(8,128)(2,1)S(1)} %bitcast.127), kind=kOutput, calls=%fused_computation.52 | convolution fusion | flops 805306368 | bytes 2359296 | tf_op jit(solution)/shard_map/while/body/eval_jaxpr/tgn,gkpn->tgkp/dot_general | solution.py:59
  97.2 16.3 %collective-permute-done.6 = bf16[128,1024]{0,1:T(8,128)(2,1)S(1)} collective-permute-done((bf16[128,1024]{0,1:T(8,128)(2,1)S(1)}, bf16[128,1024]{0,1:T(8,128)(2,1)S(1)}, u32[]{:S(2)}, u32[]{:S(2)}) %collective-permute-start.6) | collective-permute-done | bytes 262176 | tf_op jit(solution)/shard_map/ppermute | solution.py:158
  120.4 36.3 %while.38 = (s32[]{:T(128)}, f32[128,8,4]{0,2,1:T(4,128)S(1)}, f32[128,8,4]{0,2,1:T(4,128)S(1)}, f32[128,8,4,128]{0,3,2,1:T(8,128)}, bf16[1024,1024]{0,1:T(8,128...) while((s32[]{:T(128)}, f32[128,8,4]{0,2,1:T(4,128)S(1)}, ...), condition=%wide.region_7.8_spmd.clone, body=%wide.region_4.7_spmd.clone.sunk | while | flops 1102664320 | bytes 70784216 | solution.py:178
  120.4 2.6 %constant_dynamic-slice_fusion.4 = (bf16[512,1024]{0,1:T(8,128)(2,1)}, bf16[512,1024]{0,1:T(8,128)(2,1)S(1)}) fusion(bf16[1024,1024]{0,1:T(8,128)(2,1)} %get-tuple-element.512, s32[]{:T(128)S(6)} %select_n.111, bf16[1024,1024]{0,1:T(8,128)(2,1)} %get-tuple-element.510), kind=kLoop, calls=%fused_computation.20.clone.1 | loop fusion | bytes 4194308 | tf_op jit(solution)/shard_map/while/body/eval_jaxpr/dynamic_slice | solution.py:167
  123.2 4.7 %fusion.68 = (f32[128,8,4]{0,2,1:T(4,128)S(1)}, f32[8,512,128,4]{2,1,3,0:T(8,128)}) fusion(pred[128,512]{0,1:T(8,128)(4,1)S(1)} %broadcast_compare_fusion.2, bf16[512,8,128,1]{0,2,3,1:T(8,128)(2,1)S(1)} %bitcast.122, bf16[128,8,4,128]{3,0,2,1:T(8,128)(2,1)S(1)} %get-tuple-element.511), kind=kOutput, calls=%fused_computation.6.clone.1 | convolution fusion | flops 543158272 | bytes 10567680 | tf_op jit(solution)/shard_map/while/body/eval_jaxpr/qgkd,sgd->qgks/dot_general | solution.py:85
  127.9 4.7 %fusion.69 = f32[128,8,4]{0,2,1:T(4,128)S(1)} fusion(f32[8,512,128,4]{2,1,3,0:T(8,128)} %get-tuple-element.457, f32[128,8,4]{0,2,1:T(4,128)S(1)} %select_maximum_fusion.2, pred[128,512]{0,1:T(8,128)(4,1)S(1)} %broadcast_compare_fusion.2), kind=kLoop, calls=%fused_computation.8.clone.1 | loop fusion | flops 10481664 | bytes 8486912 | tf_op jit(solution)/shard_map/while/body/eval_jaxpr/reduce_sum | solution.py:94
  133.8 4.6 %bitcast_add_fusion.2 = f32[128,8,4,128]{0,3,2,1:T(8,128)} fusion(f32[128,8,4,128]{0,3,2,1:T(8,128)} %get-tuple-element.497, bf16[512,8,128,1]{0,2,3,1:T(8,128)(2,1)} %bitcast.124, f32[8,512,128,4]{2,1,3,0:T(8,128)S(1)} %copy-done, f32[128,8,4]{0,2,1:T(4,128)S(1)} %select_maximum_fusion.2, pred[128,512]{0,1:T(8,128)(4,1)S(1)} %broadcast_compare_fusion.2, ...), kind=kOutput, calls=%fused_computation.11.clone.1 | convolution fusion | flops 548929536 | bytes 13729793 | tf_op jit(solution)/shard_map/while/body/eval_jaxpr/qgks,sgd->qgkd/dot_general | solution.py:95
  138.4 2.6 %constant_dynamic-slice_fusion.4 = (bf16[512,1024]{0,1:T(8,128)(2,1)}, bf16[512,1024]{0,1:T(8,128)(2,1)S(1)}) fusion(bf16[1024,1024]{0,1:T(8,128)(2,1)} %get-tuple-element.512, s32[]{:T(128)S(6)} %select_n.111, bf16[1024,1024]{0,1:T(8,128)(2,1)} %get-tuple-element.510), kind=kLoop, calls=%fused_computation.20.clone.1 | loop fusion | bytes 4194308 | tf_op jit(solution)/shard_map/while/body/eval_jaxpr/dynamic_slice | solution.py:167
  141.2 4.7 %fusion.68 = (f32[128,8,4]{0,2,1:T(4,128)S(1)}, f32[8,512,128,4]{2,1,3,0:T(8,128)}) fusion(pred[128,512]{0,1:T(8,128)(4,1)S(1)} %broadcast_compare_fusion.2, bf16[512,8,128,1]{0,2,3,1:T(8,128)(2,1)S(1)} %bitcast.122, bf16[128,8,4,128]{3,0,2,1:T(8,128)(2,1)S(1)} %get-tuple-element.511), kind=kOutput, calls=%fused_computation.6.clone.1 | convolution fusion | flops 543158272 | bytes 10567680 | tf_op jit(solution)/shard_map/while/body/eval_jaxpr/qgkd,sgd->qgks/dot_general | solution.py:85
  146.0 4.7 %fusion.69 = f32[128,8,4]{0,2,1:T(4,128)S(1)} fusion(f32[8,512,128,4]{2,1,3,0:T(8,128)} %get-tuple-element.457, f32[128,8,4]{0,2,1:T(4,128)S(1)} %select_maximum_fusion.2, pred[128,512]{0,1:T(8,128)(4,1)S(1)} %broadcast_compare_fusion.2), kind=kLoop, calls=%fused_computation.8.clone.1 | loop fusion | flops 10481664 | bytes 8486912 | tf_op jit(solution)/shard_map/while/body/eval_jaxpr/reduce_sum | solution.py:94
  151.8 4.9 %bitcast_add_fusion.2 = f32[128,8,4,128]{0,3,2,1:T(8,128)} fusion(f32[128,8,4,128]{0,3,2,1:T(8,128)} %get-tuple-element.497, bf16[512,8,128,1]{0,2,3,1:T(8,128)(2,1)} %bitcast.124, f32[8,512,128,4]{2,1,3,0:T(8,128)S(1)} %copy-done, f32[128,8,4]{0,2,1:T(4,128)S(1)} %select_maximum_fusion.2, pred[128,512]{0,1:T(8,128)(4,1)S(1)} %broadcast_compare_fusion.2, ...), kind=kOutput, calls=%fused_computation.11.clone.1 | convolution fusion | flops 548929536 | bytes 13729793 | tf_op jit(solution)/shard_map/while/body/eval_jaxpr/qgks,sgd->qgkd/dot_general | solution.py:95
  156.7 1.8 divide_convert_fusion
  159.9 14.5 %while.37 = (s32[]{:T(128)}, f32[64,64,128]{2,1,0:T(8,128)S(1)}, s32[]{:T(128)}, bf16[8,64]{1,0:T(8,128)(2,1)S(1)}, bf16[8,64,64,128]{3,2,1,0:T(8,128)(2,1)}, /*index=5*/s32[]{:T(128)}, s32[]{:T(128)}) while((s32[]{:T(128)}, f32[64,64,128]{2,1,0:T(8,128)S(1)}, s32[]{:T(128)}, bf16[8,64]{1,0:T(8,128)(2,1)S(1)}, ...), condition=%wide.region_2.3_spmd.clone, body=%wide.region_1.2_spmd.clone.sunk | while | flops 2621508 | bytes 5243625 | solution.py:35
  159.9 1.9 fusion.63
  161.8 1.8 fusion.63
  163.6 1.8 fusion.63
  165.4 1.8 fusion.63
  167.2 1.8 fusion.63
  169.1 1.8 fusion.63
  170.9 1.8 fusion.63
  174.5 4.3 %multiply_reduce_fusion = (f32[128,8,8]{0,2,1:T(8,128)S(1)}, f32[128,8,8,64]{0,3,2,1:T(8,128)S(1)}) fusion(bf16[128,4096]{0,1:T(8,128)(2,1)S(1)} %copy-done.1, f32[8,8,64,128]{3,2,1,0:T(8,128)S(1)} %bitcast.123, bf16[128,8,128,1]{2,1,0,3:T(8,128)(2,1)S(1)} %bitcast.128, f32[128,8,8]{0,2,1:T(8,128)S(1)} %get-tuple-element.365, ...), kind=kOutput, calls=%fused_computation.41 | convolution fusion | flops 811589632 | bytes 9764864 | tf_op jit(solution)/shard_map/tgn,gkpn->tgkp/dot_general | solution.py:187
  (109 shorter events, 27.1 us)
Async XLA Ops:
  7.2 8.7 %copy-start.12 = (bf16[128,1024]{1,0:T(8,128)(2,1)S(1)}, bf16[128,1024]{1,0:T(8,128)(2,1)}, u32[]{:S(2)}) copy-start(bf16[128,1024]{1,0:T(8,128)(2,1)} %param.23) | copy-start | bytes 786436
  7.2 43.9 %copy-start.4 = (bf16[128,4096]{1,0:T(8,128)(2,1)S(1)}, bf16[128,4096]{1,0:T(8,128)(2,1)}, u32[]{:S(2)}) copy-start(bf16[128,4096]{1,0:T(8,128)(2,1)} %param.21) | copy-start | bytes 3145732
  7.2 113.2 %all-gather.6.cloned.1.call-start = ((), (), s32[]{:S(2)}) async-start(), calls=%async_computation.1 | async-start | bytes 2359296 | tf_op jit(solution)/shard_map/all_gather | solution.py:155
  9.2 150.7 %all-gather.4.cloned.1.call-start = ((), (), s32[]{:S(2)}) async-start(), calls=%async_computation | async-start | bytes 9437184 | tf_op jit(solution)/shard_map/all_gather | solution.py:18
  12.3 38.7 %copy-start.5 = (bf16[128,4096]{0,1:T(8,128)(2,1)}, bf16[128,4096]{0,1:T(8,128)(2,1)S(1)}, u32[]{:S(2)}) copy-start(bf16[128,4096]{0,1:T(8,128)(2,1)S(1)} %copy.43) | copy-start | bytes 3145732
  13.5 40.5 %copy-start.14 = (u32[32]{0:T(128)S(1)}, u32[32]{0:T(128)}, u32[]{:S(2)}) copy-start(u32[32]{0:T(128)} %constant.143) | copy-start | bytes 388
  16.0 11.5 %collective-permute-start = (bf16[128,1024]{0,1:T(8,128)(2,1)S(1)}, bf16[128,1024]{0,1:T(8,128)(2,1)S(1)}, u32[]{:S(2)}, u32[]{:S(2)}) collective-permute-start(bf16[128,1024]{0,1:T(8,128)(2,1)S(1)} %copy.50), channel_id=1, source_target_pairs={{0,1},{1,2},{2,3},{3,4},{4,5},{5,6},{6,7},{7,0},{8,9},{9,10},{10,1... | collective-permute-start | bytes 786440 | tf_op jit(solution)/shard_map/ppermute | solution.py:158
  27.5 23.5 %copy-start.6 = (bf16[128,1024]{0,1:T(8,128)(2,1)}, bf16[128,1024]{0,1:T(8,128)(2,1)S(1)}, u32[]{:S(2)}) copy-start(bf16[128,1024]{0,1:T(8,128)(2,1)S(1)} %collective-permute-done) | copy-start | bytes 786436
  27.5 8.7 %collective-permute-start.1 = (bf16[128,1024]{0,1:T(8,128)(2,1)S(1)}, bf16[128,1024]{0,1:T(8,128)(2,1)S(1)}, u32[]{:S(2)}, u32[]{:S(2)}) collective-permute-start(bf16[128,1024]{0,1:T(8,128)(2,1)S(1)} %collective-permute-done), channel_id=1, source_target_pairs={{0,1},{1,2},{2,3},{3,4},{4,5},{5,6},{6,7},{7,0},{8,9},{9,10},{10,1... | collective-permute-start | bytes 786440 | tf_op jit(solution)/shard_map/ppermute | solution.py:158
  36.2 14.8 %copy-start.8 = (bf16[128,1024]{0,1:T(8,128)(2,1)}, bf16[128,1024]{0,1:T(8,128)(2,1)S(1)}, u32[]{:S(2)}) copy-start(bf16[128,1024]{0,1:T(8,128)(2,1)S(1)} %collective-permute-done.1) | copy-start | bytes 786436
  36.2 8.8 %collective-permute-start.2 = (bf16[128,1024]{0,1:T(8,128)(2,1)S(1)}, bf16[128,1024]{0,1:T(8,128)(2,1)S(1)}, u32[]{:S(2)}, u32[]{:S(2)}) collective-permute-start(bf16[128,1024]{0,1:T(8,128)(2,1)S(1)} %collective-permute-done.1), channel_id=1, source_target_pairs={{0,1},{1,2},{2,3},{3,4},{4,5},{5,6},{6,7},{7,0},{8,9},{9,10},{10,1... | collective-permute-start | bytes 786440 | tf_op jit(solution)/shard_map/ppermute | solution.py:158
  45.0 6.0 %copy-start.10 = (bf16[128,1024]{0,1:T(8,128)(2,1)}, bf16[128,1024]{0,1:T(8,128)(2,1)S(1)}, u32[]{:S(2)}) copy-start(bf16[128,1024]{0,1:T(8,128)(2,1)S(1)} %collective-permute-done.2) | copy-start | bytes 786436
  45.0 5.9 %collective-permute-start.3 = (bf16[128,1024]{0,1:T(8,128)(2,1)S(1)}, bf16[128,1024]{0,1:T(8,128)(2,1)}, u32[]{:S(2)}, u32[]{:S(2)}) collective-permute-start(bf16[128,1024]{0,1:T(8,128)(2,1)S(1)} %collective-permute-done.2), channel_id=1, source_target_pairs={{0,1},{1,2},{2,3},{3,4},{4,5},{5,6},{6,7},{7,0},{8,9},{9,10},{10,1... | collective-permute-start | bytes 786440 | tf_op jit(solution)/shard_map/ppermute | solution.py:158
  50.9 26.9 %collective-permute-start.4 = (bf16[128,1024]{0,1:T(8,128)(2,1)}, bf16[128,1024]{0,1:T(8,128)(2,1)}, u32[]{:S(2)}, u32[]{:S(2)}) collective-permute-start(bf16[128,1024]{0,1:T(8,128)(2,1)} %collective-permute-done.3), channel_id=1, source_target_pairs={{0,1},{1,2},{2,3},{3,4},{4,5},{5,6},{6,7},{7,0},{8,9},{9,10},{10,1... | collective-permute-start | bytes 786440 | tf_op jit(solution)/shard_map/ppermute | solution.py:158
  76.4 18.4 %copy-start.2 = (bf16[16,8,8,128]{3,2,1,0:T(8,128)(2,1)S(1)}, bf16[16,8,8,128]{3,2,1,0:T(8,128)(2,1)}, u32[]{:S(2)}) copy-start(bf16[16,8,8,128]{3,2,1,0:T(8,128)(2,1)} %copy.73) | copy-start | bytes 786436
  77.8 17.1 %collective-permute-start.5 = (bf16[128,1024]{0,1:T(8,128)(2,1)}, bf16[128,1024]{0,1:T(8,128)(2,1)S(1)}, u32[]{:S(2)}, u32[]{:S(2)}) collective-permute-start(bf16[128,1024]{0,1:T(8,128)(2,1)} %collective-permute-done.4), channel_id=1, source_target_pairs={{0,1},{1,2},{2,3},{3,4},{4,5},{5,6},{6,7},{7,0},{8,9},{9,10},{10,1... | collective-permute-start | bytes 786440 | tf_op jit(solution)/shard_map/ppermute | solution.py:158
  77.9 37.9 %copy-start.11 = (bf16[128,1024]{0,1:T(8,128)(2,1)S(1)}, bf16[128,1024]{0,1:T(8,128)(2,1)}, u32[]{:S(2)}) copy-start(bf16[128,1024]{0,1:T(8,128)(2,1)} %copy-done.10) | copy-start | bytes 786436
  81.8 34.1 %copy-start.9 = (bf16[128,1024]{0,1:T(8,128)(2,1)S(1)}, bf16[128,1024]{0,1:T(8,128)(2,1)}, u32[]{:S(2)}) copy-start(bf16[128,1024]{0,1:T(8,128)(2,1)} %copy-done.8) | copy-start | bytes 786436
  81.8 34.2 %copy-start.7 = (bf16[128,1024]{0,1:T(8,128)(2,1)S(1)}, bf16[128,1024]{0,1:T(8,128)(2,1)}, u32[]{:S(2)}) copy-start(bf16[128,1024]{0,1:T(8,128)(2,1)} %copy-done.6) | copy-start | bytes 786436
  94.9 18.6 %collective-permute-start.6 = (bf16[128,1024]{0,1:T(8,128)(2,1)S(1)}, bf16[128,1024]{0,1:T(8,128)(2,1)S(1)}, u32[]{:S(2)}, u32[]{:S(2)}) collective-permute-start(bf16[128,1024]{0,1:T(8,128)(2,1)S(1)} %collective-permute-done.5), channel_id=1, source_target_pairs={{0,1},{1,2},{2,3},{3,4},{4,5},{5,6},{6,7},{7,0},{8,9},{9,10},{10,1... | collective-permute-start | bytes 786440 | tf_op jit(solution)/shard_map/ppermute | solution.py:158
  127.9 5.9 %copy-start = (f32[8,512,128,4]{2,1,3,0:T(8,128)S(1)}, f32[8,512,128,4]{2,1,3,0:T(8,128)}, u32[]{:S(2)}) copy-start(f32[8,512,128,4]{2,1,3,0:T(8,128)} %get-tuple-element.457) | copy-start | bytes 25165828 | tf_op jit(solution)/shard_map/while
  146.0 5.8 %copy-start = (f32[8,512,128,4]{2,1,3,0:T(8,128)S(1)}, f32[8,512,128,4]{2,1,3,0:T(8,128)}, u32[]{:S(2)}) copy-start(f32[8,512,128,4]{2,1,3,0:T(8,128)} %get-tuple-element.457) | copy-start | bytes 25165828 | tf_op jit(solution)/shard_map/while
  159.9 14.5 %copy-start.1 = (bf16[128,4096]{0,1:T(8,128)(2,1)S(1)}, bf16[128,4096]{0,1:T(8,128)(2,1)}, u32[]{:S(2)}) copy-start(bf16[128,4096]{0,1:T(8,128)(2,1)} %copy.47) | copy-start | bytes 3145732
  159.9 14.6 %copy-start.3 = (bf16[16,8,8,128]{3,2,1,0:T(8,128)(2,1)S(1)}, bf16[16,8,8,128]{3,2,1,0:T(8,128)(2,1)}, u32[]{:S(2)}) copy-start(bf16[16,8,8,128]{3,2,1,0:T(8,128)(2,1)} %copy.73) | copy-start | bytes 786436
  174.5 4.3 %copy-start.13 = (f32[4096]{0:T(1024)S(1)}, f32[4096]{0:T(1024)}, u32[]{:S(2)}) copy-start(f32[4096]{0:T(1024)} %param.20) | copy-start | bytes 49156
Sparse Core Ops, SparseCore 0:
  9.6 35.7 all-gather.5
  47.0 87.1 all-gather.3
